TPU v7x, 256 devices: a whole 4x4x8 slice. The times are simulated.
256 devices in a mesh: term: 8 (over y, core), pass: 32 (over x, z).
Axes of the slice: x: 4, y: 4, z: 8, core: 2. Of those that a mesh axis runs over, the one named last changes fastest.
Arguments:
- hidden: bfloat16 [16384, 4096], P('pass', 'term'), may hold values from -16 to 16
- head_weight: bfloat16 [4096, 16384], P('pass', 'term'), may hold values from -0.09375 to 0.09375
- lengths: int32 [256], P('pass'), may hold values from 1 to 64, as said below
Outputs:
- postings: bfloat16 [16384, 256], P(('term', 'pass'))
Inputs may be any that keep to these rules, and one draw needn't show every extreme that they name: Passage p's valid tokens are its first lengths[p] slots; some passage has exactly 64.
All inputs are finite; a program needn't handle non-finite values.
Results may differ from a plain program's by a relative error of at most 0.013.
Values may be sent and summed in bfloat16 or wider, within the bound.
No kernel may reach another device: no remote copies, remote signals or barrier semaphores. Data moves between devices by JAX's collectives and lax.ppermute only.
A program may use at most 64 MiB of HBM per device.

v0:
```python
import jax
import jax.numpy as jnp
from jax import lax
from jax.sharding import PartitionSpec as P


def body(hidden, head_weight, lengths):
    gathered = lax.all_gather(hidden, "term", axis=1, tiled=True)
    passages = lengths.shape[0]
    tokens_per = gathered.shape[0] // passages
    slab_cols = head_weight.shape[1]
    allowed = jnp.arange(tokens_per, dtype=jnp.int32)[None, :] < lengths[:, None]
    logits = jnp.dot(
        gathered,
        lax.all_gather(head_weight, "pass", axis=0, tiled=True),
        preferred_element_type=jnp.float32,
    )
    impacts = jnp.log1p(jnp.maximum(logits, jnp.float32(0.0)))
    impacts = impacts.reshape(passages, tokens_per, slab_cols)
    impacts = jnp.where(allowed[:, :, None], impacts, jnp.float32(0.0))
    pooled = jnp.max(impacts, axis=1).astype(jnp.bfloat16)
    owners = lax.axis_size("pass")
    range_cols = slab_cols // owners
    local_max = jnp.max(pooled.astype(jnp.float32), axis=0)
    column_max = lax.pmax(local_max, "pass")
    payload = (pooled.astype(jnp.float32) / (1.0 + column_max)[None, :]).astype(jnp.bfloat16)
    shaped = payload.reshape(passages, owners, range_cols)
    return jnp.transpose(
        lax.all_to_all(shaped, "pass", split_axis=1, concat_axis=0, tiled=True)[:, 0, :]
    )


def solution(mesh):
    return jax.shard_map(
        body,
        mesh=mesh,
        in_specs=(P("pass", "term"), P("pass", "term"), P("pass")),
        out_specs=P(("term", "pass"), None),
        check_vma=False,
    )
```

profile of v0, /device:TPU:8, one launch (start us, length us, event | category | flops | bytes accessed | tf_op | source)
XLA Modules:
  0.0 297.9 jit_solution(6542916140701454250)
XLA Ops:
  6.5 0.0 all-gather.3.cloned.1.call-start
  6.5 0.7 all-gather.3.cloned.1.call-update
  7.3 0.0 all-gather.5.cloned.1.call-start
  7.3 0.7 all-gather.5.cloned.1.call-update
  8.0 0.7 iota_compare_fusion
  8.7 37.0 %all-gather.3.cloned.1.call-done = bf16[512,4096]{1,0:T(8,128)(2,1)} async-done(((bf16[512,512]{1,0:T(8,128)(2,1)}), bf16[512,4096]{1,0:T(8,128)(2,1)}) %all-gather.3.cloned.1.call-update) | async-done | bytes 4194320 | tf_op jit(solution)/shard_map/all_gather | solution.py:8
  45.8 144.1 %all-gather.5.cloned.1.call-done = bf16[4096,2048]{1,0:T(8,128)(2,1)} async-done(((bf16[128,2048]{1,0:T(8,128)(2,1)}), bf16[4096,2048]{1,0:T(8,128)(2,1)}) %all-gather.5.cloned.1.call-update) | async-done | bytes 16777232 | tf_op jit(solution)/shard_map/all_gather | solution.py:15
  189.9 14.8 %select_reduce_fusion = bf16[8,2048]{1,0:T(8,128)(2,1)S(1)} fusion(pred[8,64]{1,0:T(8,128)(4,1)S(1)} %iota_compare_fusion, bf16[512,4096]{1,0:T(8,128)(2,1)} %all-gather.3.cloned.1.call-done, bf16[4096,2048]{1,0:T(8,128)(2,1)} %all-gather.5.cloned.1.call-done), kind=kOutput, calls=%fused_computation | convolution fusion | flops 8594112512 | bytes 21004800 | tf_op jit(solution)/shard_map/dot_general | solution.py:13
  204.8 0.1 reshape.37
  204.9 72.3 %pmax.7 = f32[2048]{0:T(1024)S(1)} all-reduce(bf16[2048]{0:T(1024)(128)(2,1)S(1)} %convert_reduce_fusion), channel_id=1, replica_groups=mesh['term'=8,'pass'=32] {'pass'}, use_global_device_ids=true, to_apply=%region_2.3 | all-reduce | flops 2048 | bytes 12288 | tf_op jit(solution)/shard_map/pmax | solution.py:25
  277.2 0.1 div.11
  277.3 0.1 reshape.38
  277.4 12.8 %all_to_all.15 = bf16[32,2,256]{2,1,0:T(2,128)(2,1)S(1)} all-to-all(bf16[32,2,256]{2,1,0:T(2,128)(2,1)S(1)} %reshape.38), channel_id=1, replica_groups=mesh['term'=8,'pass'=32] {'pass'}, dimensions={0} | all-to-all | bytes 65536 | tf_op jit(solution)/shard_map/all_to_all | solution.py:29
  290.2 0.1 reshape.39
  290.4 0.7 copy.7
  (5 shorter events, 0.1 us)
Async XLA Ops:
  6.5 39.2 %all-gather.3.cloned.1.call-start = ((), (), s32[]{:S(2)}) async-start(), calls=%async_computation.1 | async-start | bytes 4718592 | tf_op jit(solution)/shard_map/all_gather | solution.py:8
  7.3 182.6 %all-gather.5.cloned.1.call-start = ((), (), s32[]{:S(2)}) async-start(), calls=%async_computation.2 | async-start | bytes 17301504 | tf_op jit(solution)/shard_map/all_gather | solution.py:15
Sparse Core Ops, SparseCore 0:
  9.2 36.5 all-gather.2
  48.4 141.4 all-gather.4
where the time goes:
time: 298 us
  waiting for transfers between devices  183 us (61%)
  blocking collectives  85.1 us (29%)
  matrix products  14.8 us (5%)
  between operations  13.5 us (5%)
    all_gather x1, waiting for transfers between devices, body(): lax.all_gather(head_weight, 'pass', axis=0, tiled=True)  144 us
    pmax x1, blocking collectives, body(): column_max = lax.pmax(local_max, 'pass')  72.3 us
    all_gather x1, waiting for transfers between devices, body(): gathered = lax.all_gather(hidden, 'term', axis=1, tiled=True)  37 us
    dot_general x1, matrix products, body(): jnp.dot(gathered, lax.all_gather(head_weight, 'pass', axis=0, tiled=True)...  14.8 us
    all_to_all x1, blocking collectives, body(): lax.all_to_all(shaped, 'pass', split_axis=1, concat_axis=0, tiled=True)  12.8 us
  transfers between devices with their start and end apart: 2, of which 2 were waited for; matrix products, arithmetic and copies ran while one was open for 0% of the time, Pallas kernels for 0%

commit v1 on v0

--- a/solution.py
+++ b/solution.py
@@ -5,7 +5,13 @@
 
 
 def body(hidden, head_weight, lengths):
-    gathered = lax.all_gather(hidden, "term", axis=1, tiled=True)
+    peers = lax.axis_size("term")
+    moving, blocks = (hidden, [hidden])
+    for _ in range(peers - 1):
+        moving = lax.ppermute(moving, "term", [(i, (i + 1) % peers) for i in range(peers)])
+        blocks.insert(0, moving)
+    merged = jnp.concatenate(blocks, axis=1)
+    gathered = jnp.roll(merged, (lax.axis_index("term") + 1) * hidden.shape[1], axis=1)
     passages = lengths.shape[0]
     tokens_per = gathered.shape[0] // passages
     slab_cols = head_weight.shape[1]

time: 298 us -> 262 us (0.88)
  waiting for transfers between devices: 183 us -> 127 us
  local copies, waits for them, and re-layouts: 1.16 us -> 20.6 us
    all_gather x1, waiting for transfers between devices: 144 us -> 65.7 us  [body(): lax.all_gather(head_weight, 'pass', axis=0, tiled=True)]
    ppermute x0 -> x7, waiting for transfers between devices: none -> 60.1 us  [body(): lax.ppermute(moving, 'term', [(i, (i + 1) % peers) for i in range(peers)])]
    all_gather x1 -> x0, waiting for transfers between devices: 37 us -> none  [body(): gathered = lax.all_gather(hidden, 'term', axis=1, tiled=True)]
    unnamed x2 -> x19, local copies, waits for them, and re-layouts: 0.22 us -> 18.8 us
  transfers between devices with their start and end apart: 2 -> 8, of which waited for: 2 -> 8; matrix products, arithmetic and copies ran while one was open for 0% -> 8% of each run, Pallas kernels for 0% -> 0%
where the time goes in v1:
time: 262 us; the launch traced here: 261 us
  waiting for transfers between devices  127 us (48%)
  blocking collectives  85.1 us (32%)
  local copies, waits for them, and re-layouts  20.6 us (8%)
  matrix products  14.8 us (6%)
  between operations  13.5 us (5%)
    pmax x1, blocking collectives, body(): column_max = lax.pmax(local_max, 'pass')  72.3 us
    all_gather x1, waiting for transfers between devices, body(): lax.all_gather(head_weight, 'pass', axis=0, tiled=True)  65.7 us
    ppermute x7, waiting for transfers between devices, body(): lax.ppermute(moving, 'term', [(i, (i + 1) % peers) for i in range(peers)])  60.1 us
    unnamed x19, local copies, waits for them, and re-layouts  18.8 us
    dot_general x1, matrix products, body(): jnp.dot(gathered, lax.all_gather(head_weight, 'pass', axis=0, tiled=True)...  14.8 us
    all_to_all x1, blocking collectives, body(): lax.all_to_all(shaped, 'pass', split_axis=1, concat_axis=0, tiled=True)  12.8 us
  transfers between devices with their start and end apart: 8, of which 8 were waited for; matrix products, arithmetic and copies ran while one was open for 8% of the time, Pallas kernels for 0%

profile of v1, /device:TPU:8, one launch (start us, length us, event | category | flops | bytes accessed | tf_op | source)
XLA Modules:
  0.0 261.4 jit_solution(5148266944038984518)
XLA Ops:
  6.5 0.7 all-gather.2.cloned.1.call-update
  7.3 8.8 %collective-permute-done = bf16[512,512]{1,0:T(8,128)(2,1)S(1)} collective-permute-done((bf16[512,512]{1,0:T(8,128)(2,1)}, bf16[512,512]{1,0:T(8,128)(2,1)S(1)}, u32[]{:S(2)}, u32[]{:S(2)}) %collective-permute-start) | collective-permute-done | bytes 524320 | tf_op jit(solution)/shard_map/ppermute | solution.py:11
  16.1 8.6 %collective-permute-done.1 = bf16[512,512]{1,0:T(8,128)(2,1)S(1)} collective-permute-done((bf16[512,512]{1,0:T(8,128)(2,1)S(1)}, bf16[512,512]{1,0:T(8,128)(2,1)S(1)}, u32[]{:S(2)}, u32[]{:S(2)}) %collective-permute-start.1) | collective-permute-done | bytes 524320 | tf_op jit(solution)/shard_map/ppermute | solution.py:11
  24.7 8.6 %collective-permute-done.2 = bf16[512,512]{1,0:T(8,128)(2,1)S(1)} collective-permute-done((bf16[512,512]{1,0:T(8,128)(2,1)S(1)}, bf16[512,512]{1,0:T(8,128)(2,1)S(1)}, u32[]{:S(2)}, u32[]{:S(2)}) %collective-permute-start.2) | collective-permute-done | bytes 524320 | tf_op jit(solution)/shard_map/ppermute | solution.py:11
  33.3 8.6 %collective-permute-done.3 = bf16[512,512]{1,0:T(8,128)(2,1)S(1)} collective-permute-done((bf16[512,512]{1,0:T(8,128)(2,1)S(1)}, bf16[512,512]{1,0:T(8,128)(2,1)S(1)}, u32[]{:S(2)}, u32[]{:S(2)}) %collective-permute-start.3) | collective-permute-done | bytes 524320 | tf_op jit(solution)/shard_map/ppermute | solution.py:11
  41.9 8.6 %collective-permute-done.4 = bf16[512,512]{1,0:T(8,128)(2,1)S(1)} collective-permute-done((bf16[512,512]{1,0:T(8,128)(2,1)S(1)}, bf16[512,512]{1,0:T(8,128)(2,1)S(1)}, u32[]{:S(2)}, u32[]{:S(2)}) %collective-permute-start.4) | collective-permute-done | bytes 524320 | tf_op jit(solution)/shard_map/ppermute | solution.py:11
  50.5 8.7 %collective-permute-done.5 = bf16[512,512]{1,0:T(8,128)(2,1)} collective-permute-done((bf16[512,512]{1,0:T(8,128)(2,1)S(1)}, bf16[512,512]{1,0:T(8,128)(2,1)}, u32[]{:S(2)}, u32[]{:S(2)}) %collective-permute-start.5) | collective-permute-done | bytes 524320 | tf_op jit(solution)/shard_map/ppermute | solution.py:11
  59.2 0.7 iota_compare_fusion
  60.0 8.2 %collective-permute-done.6 = bf16[512,512]{1,0:T(8,128)(2,1)} collective-permute-done((bf16[512,512]{1,0:T(8,128)(2,1)}, bf16[512,512]{1,0:T(8,128)(2,1)}, u32[]{:S(2)}, u32[]{:S(2)}) %collective-permute-start.6) | collective-permute-done | bytes 524320 | tf_op jit(solution)/shard_map/ppermute | solution.py:11
  68.1 2.0 constant_dynamic-update-slice_fusion.15
  70.2 1.9 constant_dynamic-update-slice_fusion.14
  72.1 0.8 constant_dynamic-update-slice_fusion.13
  72.9 0.9 constant_dynamic-update-slice_fusion.12
  73.8 0.9 constant_dynamic-update-slice_fusion.11
  74.6 0.8 constant_dynamic-update-slice_fusion.10
  75.5 0.9 constant_dynamic-update-slice_fusion.9
  76.3 1.9 constant_dynamic-update-slice_fusion.8
  78.3 1.9 constant_dynamic-update-slice_fusion.7
  80.2 1.9 constant_dynamic-update-slice_fusion.6
  82.1 0.9 constant_dynamic-update-slice_fusion.5
  83.0 0.9 constant_dynamic-update-slice_fusion.4
  84.0 0.9 constant_dynamic-update-slice_fusion.3
  84.8 1.0 constant_dynamic-update-slice_fusion.2
  85.8 0.9 constant_dynamic-update-slice_fusion.1
  86.7 0.9 constant_dynamic-update-slice_fusion
  87.6 65.7 %all-gather.2.cloned.1.call-done = bf16[4096,2048]{1,0:T(8,128)(2,1)} async-done(((bf16[128,2048]{1,0:T(8,128)(2,1)}), bf16[4096,2048]{1,0:T(8,128)(2,1)}) %all-gather.2.cloned.1.call-update) | async-done | bytes 16777232 | tf_op jit(solution)/shard_map/all_gather | solution.py:21
  153.4 14.8 %select_reduce_fusion = bf16[8,2048]{1,0:T(8,128)(2,1)S(1)} fusion(pred[8,64]{1,0:T(8,128)(4,1)S(1)} %iota_compare_fusion, bf16[4096,2048]{1,0:T(8,128)(2,1)} %all-gather.2.cloned.1.call-done, bf16[512,8192]{1,0:T(8,128)(2,1)} %constant_dynamic-update-slice_fusion, s32[]{:T(128)S(6)} %select_n.18), kind=kOutput, calls=%fused_computation | convolution fusion | flops 8594112512 | bytes 21004804 | tf_op jit(solution)/shard_map/dot_general | solution.py:19
  168.2 0.1 reshape.37
  168.3 72.3 %pmax.7 = f32[2048]{0:T(1024)S(1)} all-reduce(bf16[2048]{0:T(1024)(128)(2,1)S(1)} %convert_reduce_fusion), channel_id=1, replica_groups=mesh['term'=8,'pass'=32] {'pass'}, use_global_device_ids=true, to_apply=%region_2.3 | all-reduce | flops 2048 | bytes 12288 | tf_op jit(solution)/shard_map/pmax | solution.py:31
  240.8 0.1 reshape.38
  240.9 12.8 %all_to_all.15 = bf16[32,2,256]{2,1,0:T(2,128)(2,1)S(1)} all-to-all(bf16[32,2,256]{2,1,0:T(2,128)(2,1)S(1)} %reshape.38), channel_id=1, replica_groups=mesh['term'=8,'pass'=32] {'pass'}, dimensions={0} | all-to-all | bytes 65536 | tf_op jit(solution)/shard_map/all_to_all | solution.py:35
  253.8 0.7 copy.7
  (17 shorter events, 0.3 us)
Async XLA Ops:
  6.5 80.2 %copy-start = (bf16[512,512]{1,0:T(8,128)(2,1)S(1)}, bf16[512,512]{1,0:T(8,128)(2,1)}, u32[]{:S(2)}) copy-start(bf16[512,512]{1,0:T(8,128)(2,1)} %param.3) | copy-start | bytes 1572868
  6.5 146.8 %all-gather.2.cloned.1.call-start = ((), (), s32[]{:S(2)}) async-start(), calls=%async_computation.1 | async-start | bytes 17301504 | tf_op jit(solution)/shard_map/all_gather | solution.py:21
  7.3 8.8 %collective-permute-start = (bf16[512,512]{1,0:T(8,128)(2,1)}, bf16[512,512]{1,0:T(8,128)(2,1)S(1)}, u32[]{:S(2)}, u32[]{:S(2)}) collective-permute-start(bf16[512,512]{1,0:T(8,128)(2,1)} %param.3), channel_id=1, source_target_pairs={{0,32},{32,64},{64,96},{96,128},{128,160},{160,192},{192,224},{224... | collective-permute-start | bytes 1572872 | tf_op jit(solution)/shard_map/ppermute | solution.py:11
  16.1 8.6 %collective-permute-start.1 = (bf16[512,512]{1,0:T(8,128)(2,1)S(1)}, bf16[512,512]{1,0:T(8,128)(2,1)S(1)}, u32[]{:S(2)}, u32[]{:S(2)}) collective-permute-start(bf16[512,512]{1,0:T(8,128)(2,1)S(1)} %collective-permute-done), channel_id=1, source_target_pairs={{0,32},{32,64},{64,96},{96,128},{128,160},{160,192},{192,224},{224... | collective-permute-start | bytes 1572872 | tf_op jit(solution)/shard_map/ppermute | solution.py:11
  24.7 8.6 %collective-permute-start.2 = (bf16[512,512]{1,0:T(8,128)(2,1)S(1)}, bf16[512,512]{1,0:T(8,128)(2,1)S(1)}, u32[]{:S(2)}, u32[]{:S(2)}) collective-permute-start(bf16[512,512]{1,0:T(8,128)(2,1)S(1)} %collective-permute-done.1), channel_id=1, source_target_pairs={{0,32},{32,64},{64,96},{96,128},{128,160},{160,192},{192,224},{224... | collective-permute-start | bytes 1572872 | tf_op jit(solution)/shard_map/ppermute | solution.py:11
  33.3 8.6 %collective-permute-start.3 = (bf16[512,512]{1,0:T(8,128)(2,1)S(1)}, bf16[512,512]{1,0:T(8,128)(2,1)S(1)}, u32[]{:S(2)}, u32[]{:S(2)}) collective-permute-start(bf16[512,512]{1,0:T(8,128)(2,1)S(1)} %collective-permute-done.2), channel_id=1, source_target_pairs={{0,32},{32,64},{64,96},{96,128},{128,160},{160,192},{192,224},{224... | collective-permute-start | bytes 1572872 | tf_op jit(solution)/shard_map/ppermute | solution.py:11
  41.9 8.6 %collective-permute-start.4 = (bf16[512,512]{1,0:T(8,128)(2,1)S(1)}, bf16[512,512]{1,0:T(8,128)(2,1)S(1)}, u32[]{:S(2)}, u32[]{:S(2)}) collective-permute-start(bf16[512,512]{1,0:T(8,128)(2,1)S(1)} %collective-permute-done.3), channel_id=1, source_target_pairs={{0,32},{32,64},{64,96},{96,128},{128,160},{160,192},{192,224},{224... | collective-permute-start | bytes 1572872 | tf_op jit(solution)/shard_map/ppermute | solution.py:11
  50.5 8.7 %collective-permute-start.5 = (bf16[512,512]{1,0:T(8,128)(2,1)S(1)}, bf16[512,512]{1,0:T(8,128)(2,1)}, u32[]{:S(2)}, u32[]{:S(2)}) collective-permute-start(bf16[512,512]{1,0:T(8,128)(2,1)S(1)} %collective-permute-done.4), channel_id=1, source_target_pairs={{0,32},{32,64},{64,96},{96,128},{128,160},{160,192},{192,224},{224... | collective-permute-start | bytes 1572872 | tf_op jit(solution)/shard_map/ppermute | solution.py:11
  59.2 8.9 %collective-permute-start.6 = (bf16[512,512]{1,0:T(8,128)(2,1)}, bf16[512,512]{1,0:T(8,128)(2,1)}, u32[]{:S(2)}, u32[]{:S(2)}) collective-permute-start(bf16[512,512]{1,0:T(8,128)(2,1)} %collective-permute-done.5), channel_id=1, source_target_pairs={{0,32},{32,64},{64,96},{96,128},{128,160},{160,192},{192,224},{224... | collective-permute-start | bytes 1572872 | tf_op jit(solution)/shard_map/ppermute | solution.py:11
Sparse Core Ops, SparseCore 0:
  9.9 143.3 all-gather.1
